TPU v7x, 256 devices: a whole 4x4x8 slice. The times are simulated.
256 devices in a mesh: row: 16 (over z, core), col: 16 (over y, x).
Axes of the slice: x: 4, y: 4, z: 8, core: 2. Of those that a mesh axis runs over, the one named last changes fastest.
Arguments:
- points: float32 [32, 65536], P(None, ('row', 'col')), may hold values from -6 to 6
- search: float32 [96, 65536], P(None, ('row', 'col')), may hold values from -24 to 24
Outputs:
- applied: float32 [96, 65536], P(None, ('row', 'col'))
- gram_a: float32 [96, 96], replicated
- gram_b: float32 [96, 96], replicated
- q_block: float32 [32, 65536], P(None, ('row', 'col'))
All inputs are finite; a program needn't handle non-finite values.
Results may differ from a plain program's by a relative error of at most 0.00036.
Values may be sent and summed in bfloat16 or wider, within the bound.
A program may use at most 128 MiB of HBM per device.

v0:
```python
import jax
import jax.numpy as jnp
from jax import lax
from jax.sharding import PartitionSpec as P

NEV = 32


def step_width():
    return 256


def pair_tile(source_points, source_squares, target_points, target_squares, kernel_rate):
    cross_terms = lax.dot_general(
        source_points,
        target_points,
        (((0,), (0,)), ((), ())),
        precision=lax.Precision.HIGHEST,
        preferred_element_type=jnp.float32,
    )
    return jnp.exp(
        -kernel_rate * (source_squares[:, None] + target_squares[None, :] - 2.0 * cross_terms)
    )


def degree_stored(source_points, source_squares, target_points, target_squares, kernel_rate):
    span_width = source_points.shape[1]
    stride = step_width()

    def degree_add_block(step_index, carry):
        running, stored = carry
        offset = step_index * stride
        block_points = lax.dynamic_slice_in_dim(source_points, offset, stride, 1)
        block_squares = lax.dynamic_slice_in_dim(source_squares, offset, stride, 0)
        affinity = pair_tile(
            block_points, block_squares, target_points, target_squares, kernel_rate
        )
        stored = lax.dynamic_update_slice_in_dim(stored, affinity.astype(jnp.bfloat16), offset, 0)
        return (running + jnp.sum(affinity, axis=0), stored)

    zero_sums = jnp.zeros((target_points.shape[1],), jnp.float32)
    empty_tile = jnp.zeros((span_width, target_points.shape[1]), jnp.bfloat16)
    return lax.fori_loop(0, span_width // stride, degree_add_block, (zero_sums, empty_tile))


def fold_stored(stored):

    def accumulate(running, shard_piece, first_index):
        span_width = shard_piece.shape[1]
        stride = step_width()

        def accumulate_add_block(step_index, partial_value):
            offset = step_index * stride
            columns = lax.dynamic_slice_in_dim(shard_piece, offset, stride, 1)
            tile_rows = lax.dynamic_slice_in_dim(stored, offset, stride, 0)
            return partial_value + jnp.dot(columns, tile_rows, preferred_element_type=jnp.float32)

        return lax.fori_loop(0, span_width // stride, accumulate_add_block, running)

    return accumulate


def degrees_and_fold(source_points, target_points, kernel_rate):
    target_squares = jnp.sum(target_points * target_points, axis=0)
    source_squares = jnp.sum(source_points * source_points, axis=0)
    partial_value, stored = degree_stored(
        source_points, source_squares, target_points, target_squares, kernel_rate
    )
    accumulate = fold_stored(stored)
    return (partial_value, accumulate)


def per_device(points, search):
    kernel_rate = 2.0 / points.shape[0]
    target_points = lax.all_gather(points, "col", axis=1, tiled=True)
    source_points = lax.all_gather(points, "row", axis=1, tiled=True)
    partial_value, accumulate = degrees_and_fold(source_points, target_points, kernel_rate)
    degrees = lax.psum_scatter(partial_value, "col", scatter_dimension=0, tiled=True)
    inverse_root = lax.rsqrt(degrees)
    scaled = (search * inverse_root[None, :]).astype(jnp.bfloat16)
    zero_sums = jnp.zeros((search.shape[0], target_points.shape[1]), jnp.float32)
    totals = accumulate(zero_sums, lax.all_gather(scaled, "row", axis=1, tiled=True), jnp.int32(0))
    applied = (
        lax.psum_scatter(totals, "col", scatter_dimension=1, tiled=True) * inverse_root[None, :]
    )
    point_count = search.shape[1] * lax.axis_size("row") * lax.axis_size("col")
    contract = (((1,), (1,)), ((), ()))
    local_a = lax.dot_general(
        search,
        applied,
        contract,
        precision=lax.Precision.HIGHEST,
        preferred_element_type=jnp.float32,
    )
    local_b = lax.dot_general(
        search,
        search,
        contract,
        precision=lax.Precision.HIGHEST,
        preferred_element_type=jnp.float32,
    )
    sum_a, sum_b = lax.psum((local_a, local_b), ("row", "col"))
    gram_a = sum_a / point_count
    gram_b = sum_b / point_count
    factor_b = jnp.linalg.cholesky(gram_b[:NEV, :NEV])
    mapping = jax.scipy.linalg.cho_solve((factor_b, True), gram_a[:NEV, :NEV]).T
    residual = applied[:NEV] - jnp.dot(mapping, search[:NEV], precision=lax.Precision.HIGHEST)
    local_r = lax.dot_general(
        residual,
        residual,
        contract,
        precision=lax.Precision.HIGHEST,
        preferred_element_type=jnp.float32,
    )
    residual_gram = lax.psum(local_r, ("row", "col")) / point_count
    factor_r = jnp.linalg.cholesky(residual_gram)
    q_block = jax.scipy.linalg.solve_triangular(factor_r, residual, lower=True)
    return (applied, gram_a, gram_b, q_block)


def solution(mesh):
    placed = (P(None, ("row", "col")), P(None, ("row", "col")))
    return jax.shard_map(
        per_device,
        mesh=mesh,
        in_specs=placed,
        out_specs=(P(None, ("row", "col")), P(), P(), P(None, ("row", "col"))),
        check_vma=False,
    )
```

profile of v0, /device:TPU:1, one launch (start us, length us, event | category | flops | bytes accessed | tf_op | source)
XLA Modules:
  0.0 711.1 jit_solution(5972083221102079643)
XLA Ops:
  7.2 20.0 %all_gather.10 = f32[32,4096]{1,0:T(8,128)S(1)} all-gather(f32[32,256]{1,0:T(8,128)} %param.7), channel_id=1, replica_groups=mesh['row'=16,'col'=16] {'col'}, dimensions={1}, use_global_device_ids=true | all-gather | bytes 557056 | tf_op jit(solution)/shard_map/all_gather | solution.py:75
  27.2 27.3 %all_gather.9 = f32[32,4096]{1,0:T(8,128)S(1)} all-gather(f32[32,256]{1,0:T(8,128)} %param.7), channel_id=1, replica_groups=mesh['row'=16,'col'=16] {'row'}, dimensions={1}, use_global_device_ids=true | all-gather | bytes 557056 | tf_op jit(solution)/shard_map/all_gather | solution.py:76
  54.6 11.0 %broadcast_in_dim.20 = bf16[4096,4096]{1,0:T(8,128)(2,1)} broadcast(bf16[]{:T(256)} %constant.130.clone.1), dimensions={} | broadcast | bytes 33554432 | tf_op jit(solution)/shard_map/broadcast_in_dim | solution.py:42
  65.6 98.8 %while.30 = (s32[]{:T(128)}, f32[4096]{0:T(1024)S(1)}, bf16[4096,4096]{1,0:T(8,128)(2,1)}, f32[4096]{0:T(1024)S(1)}, f32[4096]{0:T(1024)S(1)}, /*index=5*/f32[32...) while((s32[]{:T(128)}, f32[4096]{0:T(1024)S(1)}, ...), condition=%wide.region_4.0_spmd.clone, body=%wide.region_2.0_spmd.clone.sunk | while | flops 408948736 | bytes 6933681 | solution.py:43
  65.6 4.6 fusion.40
  70.3 1.5 convert_dynamic-update-slice_fusion.2
  71.8 4.6 fusion.40
  76.5 1.4 convert_dynamic-update-slice_fusion.2
  78.0 4.6 fusion.40
  82.6 1.5 convert_dynamic-update-slice_fusion.2
  84.1 4.6 fusion.40
  88.7 1.5 convert_dynamic-update-slice_fusion.2
  90.3 4.6 fusion.40
  94.9 1.5 convert_dynamic-update-slice_fusion.2
  96.5 4.6 fusion.40
  101.2 1.4 convert_dynamic-update-slice_fusion.2
  102.7 4.6 fusion.40
  107.3 1.5 convert_dynamic-update-slice_fusion.2
  108.9 4.6 fusion.40
  113.5 1.5 convert_dynamic-update-slice_fusion.2
  115.0 4.6 fusion.40
  119.7 1.5 convert_dynamic-update-slice_fusion.2
  121.2 4.6 fusion.40
  125.8 1.4 convert_dynamic-update-slice_fusion.2
  127.4 4.6 fusion.40
  132.0 1.5 convert_dynamic-update-slice_fusion.2
  133.5 4.6 fusion.40
  138.1 1.5 convert_dynamic-update-slice_fusion.2
  139.7 4.6 fusion.40
  144.3 1.5 convert_dynamic-update-slice_fusion.2
  145.9 4.6 fusion.40
  150.5 1.4 convert_dynamic-update-slice_fusion.2
  152.1 4.6 fusion.40
  156.7 1.5 convert_dynamic-update-slice_fusion.2
  158.3 4.6 fusion.40
  162.9 1.5 convert_dynamic-update-slice_fusion.2
  164.3 58.1 %all-reduce = f32[4096]{0:T(1024)S(1)} all-reduce(f32[4096]{0:T(1024)S(1)} %get-tuple-element.209), channel_id=2, replica_groups=mesh['row'=16,'col'=16] {'col'}, use_global_device_ids=true, to_apply=%region_5.0.clone | all-reduce | flops 4096 | bytes 32768
  223.8 30.7 %all_gather.11 = bf16[96,4096]{1,0:T(8,128)(2,1)S(1)} all-gather(bf16[96,256]{1,0:T(8,128)(2,1)S(1)} %multiply_convert_fusion), channel_id=1, replica_groups=mesh['row'=16,'col'=16] {'row'}, dimensions={1}, use_global_device_ids=true | all-gather | bytes 835584 | tf_op jit(solution)/shard_map/all_gather | solution.py:82
  254.5 38.2 %while.31 = (s32[]{:T(128)}, f32[96,4096]{1,0:T(8,128)S(1)}, bf16[96,4096]{1,0:T(8,128)(2,1)S(1)}, bf16[4096,4096]{1,0:T(8,128)(2,1)}, s32[]{:T(128)}, /*index=5*/s32[]{:T(128)}, s32[]{:T(128)}, s32[]{:T(128)}) while((s32[]{:T(128)}, f32[96,4096]{1,0:T(8,128)S(1)}, bf16[96,4096]{1,0:T(8,128)(2,1)S(1)}, ...), condition=%wide.region_7.0_spmd.clone, body=%wide.region_6.0_spmd.clone.sunk | while | flops 202113024 | bytes 5293708 | solution.py:58
  254.5 2.3 convolution_add_fusion.2
  256.9 2.4 convolution_add_fusion.2
  259.3 2.4 convolution_add_fusion.2
  261.7 2.4 convolution_add_fusion.2
  264.0 2.4 convolution_add_fusion.2
  266.4 2.4 convolution_add_fusion.2
  268.8 2.4 convolution_add_fusion.2
  271.2 2.4 convolution_add_fusion.2
  273.6 2.4 convolution_add_fusion.2
  276.0 2.4 convolution_add_fusion.2
  278.4 2.4 convolution_add_fusion.2
  280.8 2.4 convolution_add_fusion.2
  283.1 2.4 convolution_add_fusion.2
  285.5 2.4 convolution_add_fusion.2
  287.9 2.4 convolution_add_fusion.2
  290.3 2.4 convolution_add_fusion.2
  292.7 1.1 copy-done
  294.8 69.3 %reduce-scatter.2.cloned.1.call-done = f32[96,256]{1,0:T(8,128)} async-done(((f32[96,4096]{1,0:T(8,128)}), f32[96,256]{1,0:T(8,128)}) %reduce-scatter.2.cloned.1.call-update) | async-done | bytes 98320 | tf_op jit(solution)/shard_map/reduce_scatter | solution.py:84
  364.1 0.9 broadcast_multiply_fusion
  365.9 246.6 %all-reduce.4.cloned.1.call-done = (f32[96,96]{0,1:T(8,128)}, f32[96,96]{0,1:T(8,128)}) async-done(((f32[96,96]{0,1:T(8,128)}, f32[96,96]{0,1:T(8,128)}), (f32[96,96]{0,1:T(8,128)}, f32[96,96]{0,1:T(8,128)})) %all-reduce.4.cloned.1.call-update) | async-done | bytes 73744 | tf_op jit(solution)/shard_map/psum | solution.py:102
  614.1 2.9 cholesky.44
  618.4 2.4 custom-call.13
  622.3 74.3 %psum.23 = f32[32,32]{0,1:T(8,128)S(1)} all-reduce(f32[32,32]{0,1:T(8,128)S(1)} %fusion.24), channel_id=1, replica_groups=mesh['row'=16,'col'=16] {'row','col'}, use_global_device_ids=true, to_apply=%region_13.15 | all-reduce | flops 1024 | bytes 8192 | tf_op jit(solution)/shard_map/psum | solution.py:115
  696.7 2.9 cholesky.55
  701.0 2.4 custom-call.14
  (72 shorter events, 10.6 us)
Async XLA Ops:
  7.2 356.9 %reduce-scatter.2.cloned.1.call-start = ((), (), s32[]{:S(2)}) async-start(), calls=%async_computation.1 | async-start | bytes 1671168 | tf_op jit(solution)/shard_map/reduce_scatter | solution.py:84
  65.6 156.9 %copy-start.3 = (u32[256]{0:T(256)S(1)}, u32[256]{0:T(256)}, u32[]{:S(2)}) copy-start(u32[256]{0:T(256)} %constant.134) | copy-start | bytes 3076
  65.6 158.2 %copy-start.1 = (f32[96,256]{1,0:T(8,128)S(1)}, f32[96,256]{1,0:T(8,128)}, u32[]{:S(2)}) copy-start(f32[96,256]{1,0:T(8,128)} %param.8) | copy-start | bytes 294916
  292.7 1.2 copy-start
  293.9 318.6 %all-reduce.4.cloned.1.call-start = ((), (), s32[]{:S(2)}) async-start(), calls=%async_computation.2 | async-start | bytes 196608 | tf_op jit(solution)/shard_map/psum | solution.py:102
  365.0 339.3 %copy-start.2 = (f32[96,256]{1,0:T(8,128)}, f32[96,256]{1,0:T(8,128)S(1)}, u32[]{:S(2)}) copy-start(f32[96,256]{1,0:T(8,128)S(1)} %broadcast_multiply_fusion) | copy-start | bytes 294916
Sparse Core Ops, SparseCore 0:
  294.0 70.0 reduce-scatter.1
  370.3 242.1 all-reduce.3
where the time goes:
time: 712 us; the launch traced here: 711 us
  waiting for transfers between devices  316 us (44%)
  blocking collectives  210 us (29%)
  matrix products  115 us (16%)
  local copies, waits for them, and re-layouts  39.2 us (6%)
  other arithmetic  15.3 us (2%)
  between operations  14.8 us (2%)
    psum x1, waiting for transfers between devices, per_device(): sum_a, sum_b = lax.psum((local_a, local_b), ('row', 'col'))  247 us
    psum x1, blocking collectives, per_device(): residual_gram = lax.psum(local_r, ('row', 'col')) / point_count  74.3 us
    dot_general x16, matrix products, pair_tile(): lax.dot_general(source_points, target_points, (((0,), (0,)), ((), ())), p...  73.7 us
    reduce_scatter x1, waiting for transfers between devices, per_device(): lax.psum_scatter(totals, 'col', scatter_dimension=1, tiled=True)  69.3 us
    unnamed x1, blocking collectives  58.1 us
    dot_general x16, matrix products, accumulate_add_block(): jnp.dot(columns, tile_rows, preferred_element_type=jnp.float32)  37.7 us
    all_gather x1, blocking collectives, per_device(): lax.all_gather(scaled, 'row', axis=1, tiled=True)  30.7 us
    all_gather x1, blocking collectives, per_device(): source_points = lax.all_gather(points, 'row', axis=1, tiled=True)  27.3 us
  transfers between devices with their start and end apart: 2, of which 2 were waited for; matrix products, arithmetic and copies ran while one was open for 0% of the time, Pallas kernels for 0%

commit v1 on v0

--- a/solution.py
+++ b/solution.py
@@ -99,7 +99,7 @@
         precision=lax.Precision.HIGHEST,
         preferred_element_type=jnp.float32,
     )
-    sum_a, sum_b = lax.psum((local_a, local_b), ("row", "col"))
+    sum_a, sum_b = lax.psum(lax.psum((local_a, local_b), "col"), "row")
     gram_a = sum_a / point_count
     gram_b = sum_b / point_count
     factor_b = jnp.linalg.cholesky(gram_b[:NEV, :NEV])

time: 712 us -> 668 us (0.938)
  waiting for transfers between devices: 316 us -> 270 us
    psum x1 -> x2, waiting for transfers between devices: 247 us -> 201 us  [per_device(): sum_a, sum_b = lax.psum(lax.psum((local_a, local_b), 'col'), 'row')]
  transfers between devices with their start and end apart: 2 -> 3, of which waited for: 2 -> 3; matrix products, arithmetic and copies ran while one was open for 0% -> 0% of each run, Pallas kernels for 0% -> 0%
where the time goes in v1:
time: 668 us; the launch traced here: 667 us
  waiting for transfers between devices  270 us (40%)
  blocking collectives  213 us (32%)
  matrix products  115 us (17%)
  local copies, waits for them, and re-layouts  39.2 us (6%)
  other arithmetic  15.3 us (2%)
  between operations  14.5 us (2%)
    psum x2, waiting for transfers between devices, per_device(): sum_a, sum_b = lax.psum(lax.psum((local_a, local_b), 'col'), 'row')  201 us
    psum x1, blocking collectives, per_device(): residual_gram = lax.psum(local_r, ('row', 'col')) / point_count  76.5 us
    dot_general x16, matrix products, pair_tile(): lax.dot_general(source_points, target_points, (((0,), (0,)), ((), ())), p...  73.7 us
    reduce_scatter x1, waiting for transfers between devices, per_device(): lax.psum_scatter(totals, 'col', scatter_dimension=1, tiled=True)  69.3 us
    unnamed x1, blocking collectives  58.1 us
    dot_general x16, matrix products, accumulate_add_block(): jnp.dot(columns, tile_rows, preferred_element_type=jnp.float32)  37.7 us
    all_gather x1, blocking collectives, per_device(): lax.all_gather(scaled, 'row', axis=1, tiled=True)  30.7 us
    all_gather x1, blocking collectives, per_device(): source_points = lax.all_gather(points, 'row', axis=1, tiled=True)  27.3 us
  transfers between devices with their start and end apart: 3, of which 3 were waited for; matrix products, arithmetic and copies ran while one was open for 0% of the time, Pallas kernels for 0%

profile of v1, /device:TPU:1, one launch (start us, length us, event | category | flops | bytes accessed | tf_op | source)
XLA Modules:
  0.0 667.4 jit_solution(14540982678470360163)
XLA Ops:
  7.2 20.0 %all_gather.10 = f32[32,4096]{1,0:T(8,128)S(1)} all-gather(f32[32,256]{1,0:T(8,128)} %param.7), channel_id=1, replica_groups=mesh['row'=16,'col'=16] {'col'}, dimensions={1}, use_global_device_ids=true | all-gather | bytes 557056 | tf_op jit(solution)/shard_map/all_gather | solution.py:75
  27.2 27.3 %all_gather.9 = f32[32,4096]{1,0:T(8,128)S(1)} all-gather(f32[32,256]{1,0:T(8,128)} %param.7), channel_id=1, replica_groups=mesh['row'=16,'col'=16] {'row'}, dimensions={1}, use_global_device_ids=true | all-gather | bytes 557056 | tf_op jit(solution)/shard_map/all_gather | solution.py:76
  54.6 11.0 %broadcast_in_dim.20 = bf16[4096,4096]{1,0:T(8,128)(2,1)} broadcast(bf16[]{:T(256)} %constant.130.clone.1), dimensions={} | broadcast | bytes 33554432 | tf_op jit(solution)/shard_map/broadcast_in_dim | solution.py:42
  65.6 98.8 %while.30 = (s32[]{:T(128)}, f32[4096]{0:T(1024)S(1)}, bf16[4096,4096]{1,0:T(8,128)(2,1)}, f32[4096]{0:T(1024)S(1)}, f32[4096]{0:T(1024)S(1)}, /*index=5*/f32[32...) while((s32[]{:T(128)}, f32[4096]{0:T(1024)S(1)}, ...), condition=%wide.region_4.0_spmd.clone, body=%wide.region_2.0_spmd.clone.sunk | while | flops 408948736 | bytes 6933681 | solution.py:43
  65.6 4.6 fusion.40
  70.3 1.5 convert_dynamic-update-slice_fusion.2
  71.8 4.6 fusion.40
  76.5 1.4 convert_dynamic-update-slice_fusion.2
  78.0 4.6 fusion.40
  82.6 1.5 convert_dynamic-update-slice_fusion.2
  84.1 4.6 fusion.40
  88.7 1.5 convert_dynamic-update-slice_fusion.2
  90.3 4.6 fusion.40
  94.9 1.5 convert_dynamic-update-slice_fusion.2
  96.5 4.6 fusion.40
  101.2 1.4 convert_dynamic-update-slice_fusion.2
  102.7 4.6 fusion.40
  107.3 1.5 convert_dynamic-update-slice_fusion.2
  108.9 4.6 fusion.40
  113.5 1.5 convert_dynamic-update-slice_fusion.2
  115.0 4.6 fusion.40
  119.7 1.5 convert_dynamic-update-slice_fusion.2
  121.2 4.6 fusion.40
  125.8 1.4 convert_dynamic-update-slice_fusion.2
  127.4 4.6 fusion.40
  132.0 1.5 convert_dynamic-update-slice_fusion.2
  133.5 4.6 fusion.40
  138.1 1.5 convert_dynamic-update-slice_fusion.2
  139.7 4.6 fusion.40
  144.3 1.5 convert_dynamic-update-slice_fusion.2
  145.9 4.6 fusion.40
  150.5 1.4 convert_dynamic-update-slice_fusion.2
  152.1 4.6 fusion.40
  156.7 1.5 convert_dynamic-update-slice_fusion.2
  158.3 4.6 fusion.40
  162.9 1.5 convert_dynamic-update-slice_fusion.2
  164.3 58.1 %all-reduce = f32[4096]{0:T(1024)S(1)} all-reduce(f32[4096]{0:T(1024)S(1)} %get-tuple-element.209), channel_id=2, replica_groups=mesh['row'=16,'col'=16] {'col'}, use_global_device_ids=true, to_apply=%region_5.0.clone | all-reduce | flops 4096 | bytes 32768
  223.8 30.7 %all_gather.11 = bf16[96,4096]{1,0:T(8,128)(2,1)S(1)} all-gather(bf16[96,256]{1,0:T(8,128)(2,1)S(1)} %multiply_convert_fusion), channel_id=1, replica_groups=mesh['row'=16,'col'=16] {'row'}, dimensions={1}, use_global_device_ids=true | all-gather | bytes 835584 | tf_op jit(solution)/shard_map/all_gather | solution.py:82
  254.5 38.2 %while.31 = (s32[]{:T(128)}, f32[96,4096]{1,0:T(8,128)S(1)}, bf16[96,4096]{1,0:T(8,128)(2,1)S(1)}, bf16[4096,4096]{1,0:T(8,128)(2,1)}, s32[]{:T(128)}, /*index=5*/s32[]{:T(128)}, s32[]{:T(128)}, s32[]{:T(128)}) while((s32[]{:T(128)}, f32[96,4096]{1,0:T(8,128)S(1)}, bf16[96,4096]{1,0:T(8,128)(2,1)S(1)}, ...), condition=%wide.region_7.0_spmd.clone, body=%wide.region_6.0_spmd.clone.sunk | while | flops 202113024 | bytes 5293708 | solution.py:58
  254.5 2.3 convolution_add_fusion.2
  256.9 2.4 convolution_add_fusion.2
  259.3 2.4 convolution_add_fusion.2
  261.7 2.4 convolution_add_fusion.2
  264.0 2.4 convolution_add_fusion.2
  266.4 2.4 convolution_add_fusion.2
  268.8 2.4 convolution_add_fusion.2
  271.2 2.4 convolution_add_fusion.2
  273.6 2.4 convolution_add_fusion.2
  276.0 2.4 convolution_add_fusion.2
  278.4 2.4 convolution_add_fusion.2
  280.8 2.4 convolution_add_fusion.2
  283.1 2.4 convolution_add_fusion.2
  285.5 2.4 convolution_add_fusion.2
  287.9 2.4 convolution_add_fusion.2
  290.3 2.4 convolution_add_fusion.2
  292.7 1.1 copy-done
  294.8 69.3 %reduce-scatter.2.cloned.1.call-done = f32[96,256]{1,0:T(8,128)} async-done(((f32[96,4096]{1,0:T(8,128)}), f32[96,256]{1,0:T(8,128)}) %reduce-scatter.2.cloned.1.call-update) | async-done | bytes 98320 | tf_op jit(solution)/shard_map/reduce_scatter | solution.py:84
  365.9 93.7 %all-reduce.6.cloned.1.call-done = (f32[96,96]{0,1:T(8,128)}, f32[96,96]{0,1:T(8,128)}) async-done(((f32[96,96]{0,1:T(8,128)}, f32[96,96]{0,1:T(8,128)}), (f32[96,96]{0,1:T(8,128)}, f32[96,96]{0,1:T(8,128)})) %all-reduce.6.cloned.1.call-update) | async-done | bytes 73744 | tf_op jit(solution)/shard_map/psum | solution.py:102
  459.6 107.3 %all-reduce.8.cloned.1.call-done = (f32[96,96]{0,1:T(8,128)}, f32[96,96]{0,1:T(8,128)}) async-done(((f32[96,96]{0,1:T(8,128)}, f32[96,96]{0,1:T(8,128)}), (f32[96,96]{0,1:T(8,128)}, f32[96,96]{0,1:T(8,128)})) %all-reduce.8.cloned.1.call-update) | async-done | bytes 73744 | tf_op jit(solution)/shard_map/psum | solution.py:102
  568.5 2.9 cholesky.44
  572.8 2.4 custom-call.13
  576.7 76.5 %psum.39 = f32[32,32]{0,1:T(8,128)S(1)} all-reduce(f32[32,32]{0,1:T(8,128)S(1)} %fusion.24), channel_id=1, replica_groups=mesh['row'=16,'col'=16] {'row','col'}, use_global_device_ids=true, to_apply=%region_15.17 | all-reduce | flops 1024 | bytes 8192 | tf_op jit(solution)/shard_map/psum | solution.py:115
  653.3 2.9 cholesky.55
  657.6 2.4 custom-call.14
  (75 shorter events, 11.6 us)
Async XLA Ops:
  7.2 356.9 %reduce-scatter.2.cloned.1.call-start = ((), (), s32[]{:S(2)}) async-start(), calls=%async_computation.1 | async-start | bytes 1671168 | tf_op jit(solution)/shard_map/reduce_scatter | solution.py:84
  65.6 156.9 %copy-start.3 = (u32[256]{0:T(256)S(1)}, u32[256]{0:T(256)}, u32[]{:S(2)}) copy-start(u32[256]{0:T(256)} %constant.134) | copy-start | bytes 3076
  65.6 158.2 %copy-start.1 = (f32[96,256]{1,0:T(8,128)S(1)}, f32[96,256]{1,0:T(8,128)}, u32[]{:S(2)}) copy-start(f32[96,256]{1,0:T(8,128)} %param.8) | copy-start | bytes 294916
  292.7 1.2 copy-start
  293.9 165.7 %all-reduce.6.cloned.1.call-start = ((), (), s32[]{:S(2)}) async-start(), calls=%async_computation.2 | async-start | bytes 196608 | tf_op jit(solution)/shard_map/psum | solution.py:102
  365.0 295.9 %copy-start.2 = (f32[96,256]{1,0:T(8,128)}, f32[96,256]{1,0:T(8,128)S(1)}, u32[]{:S(2)}) copy-start(f32[96,256]{1,0:T(8,128)S(1)} %broadcast_multiply_fusion) | copy-start | bytes 294916
  365.9 201.0 %all-reduce.8.cloned.1.call-start = ((), (), s32[]{:S(2)}) async-start(), calls=%async_computation.3 | async-start | bytes 196608 | tf_op jit(solution)/shard_map/psum | solution.py:102
Sparse Core Ops, SparseCore 0:
  294.0 70.0 reduce-scatter.1
  368.0 91.5 all-reduce.5
  462.1 104.6 all-reduce.7
